TPU v7x, 512 devices: a whole 4x8x8 slice. The times are simulated.
512 devices in a mesh: section: 4 (over x), sub: 32 (over z_lo, y), rng: 4 (over z_hi, core).
Axes of the slice: x: 4, y: 8, z: 8 (z_hi: 2, z_lo: 4; z = z_hi * 4 + z_lo), core: 2. Of those that a mesh axis runs over, the one named last changes fastest.
Arguments:
- echoes: bfloat16 [2, 32, 24, 16384], P(None, 'sub', 'section', 'rng'), may hold values from -6 to 6
- chirp: bfloat16 [2, 2048], replicated, may hold values from -0.25 to 0.25
- steer: bfloat16 [2, 32, 128, 24], P(None, 'sub'), may hold values from -2 to 2
- pulse_order: int32 [32, 24], P('sub'), may hold values from 0 to 23, each once within a row
- band_coef: bfloat16 [5, 32, 2, 2, 128, 16], P(None, 'sub'), may hold values from -2.5 to 2.5
- band_start: int32 [5, 32, 2, 128], P(None, 'sub'), may hold values from 0 to 112
- band_width: int32 [5, 32, 2, 128], P(None, 'sub'), may hold values from 1 to 16
Outputs:
- image: bfloat16 [2, 4096, 4, 4096], P(None, 'sub', 'rng', 'section')
Inputs may be any that keep to these rules, and one draw needn't show every extreme that they name: `pulse_order`: each row is a permutation of the 24 aperture positions.
All inputs are finite; a program needn't handle non-finite values.
Results may differ from a plain program's by a relative error of at most 0.0085.
Values may be sent and summed in bfloat16 or wider, within the bound.
A program may use at most 64 MiB of HBM per device.

v0:
```python
import jax
import jax.numpy as jnp
from jax import lax
from jax.sharding import PartitionSpec as P

CBLK = 128


def from_behind(value, axis, by):
    size = lax.axis_size(axis)
    pairs = [(i, i + by) for i in range(size) if 0 <= i + by < size]
    return lax.ppermute(value, axis, pairs)


def from_partner(block, axis, stride):
    count = lax.axis_size(axis)
    route = []
    for low in range(count):
        high = low | 1 << stride
        if high != low and high < count:
            route += [(low, high), (high, low)]
    return lax.ppermute(block, axis, route)


def band_matrix(coef_side, start_side, width_side):
    beam_count = coef_side.shape[1]
    tap_count = coef_side.shape[2]
    column = jnp.arange(beam_count, dtype=jnp.int32)
    offset = column[None, :] - start_side[:, None]
    taps = jnp.arange(tap_count, dtype=jnp.int32)
    hits = (offset[None, :, :] == taps[:, None, None]) & (
        taps[:, None, None] < width_side[None, :, None]
    )
    selector = hits.astype(jnp.bfloat16)
    return jnp.einsum(
        "sqt,tqc->sqc", coef_side, selector, preferred_element_type=jnp.float32
    ).astype(jnp.bfloat16)


def merge_level(own, partner_image, coef_level, start_level, width_level):
    self_matrix = band_matrix(coef_level[0], start_level[0], width_level[0])
    cross_matrix = band_matrix(coef_level[1], start_level[1], width_level[1])
    upper_rows = jnp.concatenate(
        [self_matrix[0], -self_matrix[1], cross_matrix[0], -cross_matrix[1]], axis=1
    )
    lower_rows = jnp.concatenate(
        [self_matrix[1], self_matrix[0], cross_matrix[1], cross_matrix[0]], axis=1
    )
    operator = jnp.concatenate([upper_rows, lower_rows], axis=0)
    stacked = jnp.concatenate([own[0], own[1], partner_image[0], partner_image[1]], axis=0)
    merged = jnp.dot(operator, stacked, preferred_element_type=jnp.float32)
    return merged.reshape(2, own.shape[1], own.shape[2]).astype(jnp.bfloat16)


def lag_tables(chirp, extra_blocks):
    tap_count = chirp.shape[1]
    padded = jnp.concatenate(
        [jnp.zeros((2, CBLK), jnp.bfloat16), chirp, jnp.zeros((2, 2 * CBLK), jnp.bfloat16)], axis=1
    )
    total_len = tap_count + 3 * CBLK
    tiled = jnp.tile(padded, (1, CBLK))[:, : CBLK * (total_len - 1)]
    shifted = tiled.reshape(2, CBLK, total_len - 1)[:, :, CBLK : CBLK + (extra_blocks + 1) * CBLK]
    shifted = shifted.reshape(2, CBLK, extra_blocks + 1, CBLK)
    return jnp.transpose(shifted, (0, 2, 3, 1))


def compress(signal, chirp):
    pulse_count = signal.shape[1]
    range_count = signal.shape[2]
    tap_count = chirp.shape[1]
    next_rim = from_behind(signal[:, :, :tap_count], "rng", -1)
    extended = jnp.concatenate([signal, next_rim], axis=2)
    block_count = range_count // CBLK
    extra_blocks = tap_count // CBLK
    blocks = extended.reshape(2, pulse_count, block_count + extra_blocks, CBLK)
    blocks = jnp.transpose(blocks, (1, 2, 0, 3)).reshape(
        pulse_count, block_count + extra_blocks, 2 * CBLK
    )
    parts_table = lag_tables(chirp, extra_blocks)
    chirp_real = parts_table[0]
    chirp_imag = parts_table[1]
    upper_rows = jnp.concatenate([chirp_real, -chirp_imag], axis=2)
    lower_rows = jnp.concatenate([chirp_imag, chirp_real], axis=2)
    tables = jnp.concatenate([upper_rows, lower_rows], axis=1)

    def add_piece(lag, accumulated):
        window = lax.dynamic_slice_in_dim(blocks, lag, block_count, 1)
        table = lax.dynamic_index_in_dim(tables, lag, 0, keepdims=False)
        return accumulated + jnp.einsum(
            "pbi,io->pbo", window, table, preferred_element_type=jnp.float32
        )

    accumulated = lax.fori_loop(
        0, extra_blocks + 1, add_piece, jnp.zeros((pulse_count, block_count, 2 * CBLK), jnp.float32)
    )
    accumulated = accumulated.reshape(pulse_count, block_count, 2, CBLK)
    return (
        jnp.transpose(accumulated, (2, 0, 1, 3))
        .reshape(2, pulse_count, range_count)
        .astype(jnp.bfloat16)
    )


def on_device(echoes, chirp, steer, pulse_order, band_coef, band_start, band_width):
    compressed = compress(echoes[:, 0], chirp)
    pulse_rows = lax.all_to_all(compressed, "section", split_axis=2, concat_axis=1, tiled=True)
    position_count = pulse_order.shape[1]
    positions = jnp.arange(position_count, dtype=jnp.int32)
    selector = (positions[:, None] == pulse_order[0][None, :]).astype(jnp.bfloat16)
    weights = jnp.einsum(
        "sqj,jk->sqk", steer[:, 0], selector, preferred_element_type=jnp.float32
    ).astype(jnp.bfloat16)
    forming = jnp.concatenate(
        [
            jnp.concatenate([weights[0], -weights[1]], axis=1),
            jnp.concatenate([weights[1], weights[0]], axis=1),
        ],
        axis=0,
    )
    stacked_rows = jnp.concatenate([pulse_rows[0], pulse_rows[1]], axis=0)
    beam_count = weights.shape[1]
    level_image = (
        jnp.dot(forming, stacked_rows, preferred_element_type=jnp.float32)
        .reshape(2, beam_count, pulse_rows.shape[2])
        .astype(jnp.bfloat16)
    )
    bit_count = lax.axis_size("sub").bit_length() - 1
    coef_all = band_coef[:, 0]
    start_all = band_start[:, 0]
    width_all = band_width[:, 0]
    section_count = coef_all.shape[0]
    for level in range(section_count):
        partner_image = from_partner(level_image, "sub", level % bit_count)
        level_image = merge_level(
            level_image, partner_image, coef_all[level], start_all[level], width_all[level]
        )
    return level_image[:, :, None, :]


def solution(mesh):
    return jax.shard_map(
        on_device,
        mesh=mesh,
        in_specs=(
            P(None, "sub", "section", "rng"),
            P(),
            P(None, "sub", None, None),
            P("sub", None),
            P(None, "sub", None, None, None, None),
            P(None, "sub", None, None),
            P(None, "sub", None, None),
        ),
        out_specs=P(None, "sub", "rng", "section"),
        check_vma=False,
    )
```

profile of v0, /device:TPU:1, one launch (start us, length us, event | category | flops | bytes accessed | tf_op | source)
XLA Modules:
  0.0 180.4 jit_solution(6251457165325808575)
XLA Ops:
  0.0 1.5 slice.437
  1.5 8.8 %collective-permute-start = (bf16[2,6,2048]{2,0,1:T(2,128)(2,1)}, bf16[2,6,2048]{2,0,1:T(2,128)(2,1)}, u32[]{:S(2)}, u32[]{:S(2)}) collective-permute-start(bf16[2,6,2048]{2,0,1:T(2,128)(2,1)} %slice.437), channel_id=1, source_target_pairs={{1,0},{2,1},{3,2},{5,4},{6,5},{7,6},{9,8},{10,9},{11,10},{13,12},{... | collective-permute-start | bytes 147464 | tf_op jit(solution)/shard_map/ppermute | solution.py:12
  11.1 1.3 copy.173
  13.3 2.1 %reshape.582 = bf16[622336]{0:T(1024)(128)(2,1)S(1)} reshape(bf16[2,311168]{1,0:T(2,128)(2,1)S(1)} %slice.438) | data formatting | bytes 2489344
  15.5 2.2 %reshape.578 = bf16[2,128,2431]{2,1,0:T(8,128)(2,1)S(1)} reshape(bf16[622336]{0:T(1024)(128)(2,1)S(1)} %reshape.582) | data formatting | bytes 2489344 | tf_op jit(solution)/shard_map/reshape | solution.py:62
  18.7 1.7 copy.133
  35.3 1.4 maximum_maximum_fusion
  37.9 4.0 %while.14 = (s32[]{:T(128)}, f32[6,32,256]{2,1,0:T(8,128)S(1)}, bf16[6,48,256]{2,1,0:T(8,128)(2,1)S(1)}, bf16[17,256,256]{2,1,0:T(8,128)(2,1)S(1)}, s32[]{:T(128)}, /*index=5*/s32[]{:T(128)}) while((s32[]{:T(128)}, f32[6,32,256]{2,1,0:T(8,128)S(1)}, bf16[6,48,256]{2,1,0:T(8,128)(2,1)S(1)}, bf16[17,256,256]{2,1,0:T(8,128)(2,1)S(1)}, ...), condition=%wide.region_1.2_spmd.clone, body=%wide.region_0.1_spmd.clone.sunk | while | flops 25264132 | bytes 623695 | solution.py:93
  41.9 1.4 copy.140
  43.3 4.2 %reshape.584 = bf16[4,2,6144]{2,1,0:T(2,128)(2,1)} reshape(bf16[4096,2,6]{2,1,0:T(2,128)(2,1)S(1)} %bitcast.228) | data formatting | bytes 196608
  47.5 3.5 %all-to-all-start = ((bf16[4,2,6144]{2,1,0:T(2,128)(2,1)}), bf16[4,2,6144]{2,1,0:T(2,128)(2,1)S(1)}, u32[]{:S(2)}, u32[]{:S(2)}) async-start(bf16[4,2,6144]{2,1,0:T(2,128)(2,1)} %reshape.584), calls=%async_computation | async-start | bytes 196608 | tf_op jit(solution)/shard_map/all_to_all | solution.py:106
  51.0 4.9 %all-to-all-done = bf16[4,2,6144]{2,1,0:T(2,128)(2,1)S(1)} async-done(((bf16[4,2,6144]{2,1,0:T(2,128)(2,1)}), bf16[4,2,6144]{2,1,0:T(2,128)(2,1)S(1)}, u32[]{:S(2)}, u32[]{:S(2)}) %all-to-all-start) | async-done | bytes 98336 | tf_op jit(solution)/shard_map/all_to_all | solution.py:106
  55.9 4.8 %reshape.585 = bf16[4096,2,6]{2,1,0:T(2,128)(2,1)S(1)} reshape(bf16[4,2,6144]{2,1,0:T(2,128)(2,1)S(1)} %all-to-all-done) | data formatting | bytes 196608
  60.7 1.5 copy.141
  62.8 1.9 %collective-permute-start.1 = (bf16[2,128,1024]{2,1,0:T(8,128)(2,1)S(1)}, bf16[2,128,1024]{2,1,0:T(8,128)(2,1)S(1)}, u32[]{:S(2)}, u32[]{:S(2)}) collective-permute-start(bf16[2,128,1024]{2,1,0:T(8,128)(2,1)S(1)} %bitcast.233), channel_id=1, source_target_pairs={{0,4},{4,0},{8,12},{12,8},{16,20},{20,16},{24,28},{28,24},{32,36},... | collective-permute-start | bytes 1572872 | tf_op jit(solution)/shard_map/ppermute | solution.py:22
  65.6 12.2 %collective-permute-done.1 = bf16[2,128,1024]{2,1,0:T(8,128)(2,1)S(1)} collective-permute-done((bf16[2,128,1024]{2,1,0:T(8,128)(2,1)S(1)}, bf16[2,128,1024]{2,1,0:T(8,128)(2,1)S(1)}, u32[]{:S(2)}, u32[]{:S(2)}) %collective-permute-start.1) | collective-permute-done | bytes 524320 | tf_op jit(solution)/shard_map/ppermute | solution.py:22
  78.4 2.1 %collective-permute-start.2 = (bf16[2,128,1024]{2,1,0:T(8,128)(2,1)S(1)}, bf16[2,128,1024]{2,1,0:T(8,128)(2,1)S(1)}, u32[]{:S(2)}, u32[]{:S(2)}) collective-permute-start(bf16[2,128,1024]{2,1,0:T(8,128)(2,1)S(1)} %bitcast.247), channel_id=1, source_target_pairs={{0,8},{8,0},{4,12},{12,4},{16,24},{24,16},{20,28},{28,20},{32,40},... | collective-permute-start | bytes 1572872 | tf_op jit(solution)/shard_map/ppermute | solution.py:22
  81.2 25.1 %collective-permute-done.2 = bf16[2,128,1024]{2,1,0:T(8,128)(2,1)S(1)} collective-permute-done((bf16[2,128,1024]{2,1,0:T(8,128)(2,1)S(1)}, bf16[2,128,1024]{2,1,0:T(8,128)(2,1)S(1)}, u32[]{:S(2)}, u32[]{:S(2)}) %collective-permute-start.2) | collective-permute-done | bytes 524320 | tf_op jit(solution)/shard_map/ppermute | solution.py:22
  107.0 3.0 %collective-permute-start.3 = (bf16[2,128,1024]{2,1,0:T(8,128)(2,1)S(1)}, bf16[2,128,1024]{2,1,0:T(8,128)(2,1)S(1)}, u32[]{:S(2)}, u32[]{:S(2)}) collective-permute-start(bf16[2,128,1024]{2,1,0:T(8,128)(2,1)S(1)} %bitcast.248), channel_id=1, source_target_pairs={{0,16},{16,0},{4,20},{20,4},{8,24},{24,8},{12,28},{28,12},{32,48},... | collective-permute-start | bytes 1572872 | tf_op jit(solution)/shard_map/ppermute | solution.py:22
  110.8 24.9 %collective-permute-done.3 = bf16[2,128,1024]{2,1,0:T(8,128)(2,1)S(1)} collective-permute-done((bf16[2,128,1024]{2,1,0:T(8,128)(2,1)S(1)}, bf16[2,128,1024]{2,1,0:T(8,128)(2,1)S(1)}, u32[]{:S(2)}, u32[]{:S(2)}) %collective-permute-start.3) | collective-permute-done | bytes 524320 | tf_op jit(solution)/shard_map/ppermute | solution.py:22
  136.2 1.9 %collective-permute-start.4 = (bf16[2,128,1024]{2,1,0:T(8,128)(2,1)S(1)}, bf16[2,128,1024]{2,1,0:T(8,128)(2,1)S(1)}, u32[]{:S(2)}, u32[]{:S(2)}) collective-permute-start(bf16[2,128,1024]{2,1,0:T(8,128)(2,1)S(1)} %bitcast.249), channel_id=1, source_target_pairs={{0,32},{32,0},{4,36},{36,4},{8,40},{40,8},{12,44},{44,12},{16,48},... | collective-permute-start | bytes 1572872 | tf_op jit(solution)/shard_map/ppermute | solution.py:22
  138.9 11.9 %collective-permute-done.4 = bf16[2,128,1024]{2,1,0:T(8,128)(2,1)S(1)} collective-permute-done((bf16[2,128,1024]{2,1,0:T(8,128)(2,1)S(1)}, bf16[2,128,1024]{2,1,0:T(8,128)(2,1)S(1)}, u32[]{:S(2)}, u32[]{:S(2)}) %collective-permute-start.4) | collective-permute-done | bytes 524320 | tf_op jit(solution)/shard_map/ppermute | solution.py:22
  151.4 3.2 %collective-permute-start.5 = (bf16[2,128,1024]{2,1,0:T(8,128)(2,1)S(1)}, bf16[2,128,1024]{2,1,0:T(8,128)(2,1)S(1)}, u32[]{:S(2)}, u32[]{:S(2)}) collective-permute-start(bf16[2,128,1024]{2,1,0:T(8,128)(2,1)S(1)} %bitcast.250), channel_id=1, source_target_pairs={{0,64},{64,0},{4,68},{68,4},{8,72},{72,8},{12,76},{76,12},{16,80},... | collective-permute-start | bytes 1572872 | tf_op jit(solution)/shard_map/ppermute | solution.py:22
  154.8 24.4 %collective-permute-done.5 = bf16[2,128,1024]{2,1,0:T(8,128)(2,1)S(1)} collective-permute-done((bf16[2,128,1024]{2,1,0:T(8,128)(2,1)S(1)}, bf16[2,128,1024]{2,1,0:T(8,128)(2,1)S(1)}, u32[]{:S(2)}, u32[]{:S(2)}) %collective-permute-start.5) | collective-permute-done | bytes 524320 | tf_op jit(solution)/shard_map/ppermute | solution.py:22
  (184 shorter events, 29.2 us)
Async XLA Ops:
  0.0 26.7 %copy-start = (bf16[2,1,128,24]{2,3,1,0:T(8,128)(2,1)S(1)}, bf16[2,1,128,24]{2,3,1,0:T(8,128)(2,1)}, u32[]{:S(2)}) copy-start(bf16[2,1,128,24]{2,3,1,0:T(8,128)(2,1)} %param.11) | copy-start | bytes 36868
  1.5 35.3 %collective-permute-start = (bf16[2,6,2048]{2,0,1:T(2,128)(2,1)}, bf16[2,6,2048]{2,0,1:T(2,128)(2,1)}, u32[]{:S(2)}, u32[]{:S(2)}) collective-permute-start(bf16[2,6,2048]{2,0,1:T(2,128)(2,1)} %slice.437), channel_id=1, source_target_pairs={{1,0},{2,1},{3,2},{5,4},{6,5},{7,6},{9,8},{10,9},{11,10},{13,12},{... | collective-permute-start | bytes 147464 | tf_op jit(solution)/shard_map/ppermute | solution.py:12
  21.5 5.2 %copy-start.34 = (s32[1,24]{1,0:T(1,128)S(1)}, s32[1,24]{1,0:T(1,128)}, u32[]{:S(2)}) copy-start(s32[1,24]{1,0:T(1,128)} %param.12) | copy-start | bytes 292
  41.9 9.0 %copy-start.24 = (bf16[2,128,24]{1,2,0:T(8,128)(2,1)S(1)}, bf16[2,128,24]{1,2,0:T(8,128)(2,1)}, u32[]{:S(2)}) copy-start(bf16[2,128,24]{1,2,0:T(8,128)(2,1)} %copy-done.23) | copy-start | bytes 36868
  47.5 8.4 %all-to-all-start = ((bf16[4,2,6144]{2,1,0:T(2,128)(2,1)}), bf16[4,2,6144]{2,1,0:T(2,128)(2,1)S(1)}, u32[]{:S(2)}, u32[]{:S(2)}) async-start(bf16[4,2,6144]{2,1,0:T(2,128)(2,1)} %reshape.584), calls=%async_computation | async-start | bytes 196608 | tf_op jit(solution)/shard_map/all_to_all | solution.py:106
  51.0 11.4 %copy-start.25 = (bf16[128,24]{0,1:T(8,128)(2,1)S(1)}, bf16[128,24]{0,1:T(8,128)(2,1)}, u32[]{:S(2)}) copy-start(bf16[128,24]{0,1:T(8,128)(2,1)} %get-tuple-element.172) | copy-start | bytes 18436
  51.0 11.4 %copy-start.26 = (bf16[128,24]{0,1:T(8,128)(2,1)S(1)}, bf16[128,24]{0,1:T(8,128)(2,1)}, u32[]{:S(2)}) copy-start(bf16[128,24]{0,1:T(8,128)(2,1)} %get-tuple-element.173) | copy-start | bytes 18436
  62.2 15.6 %copy-start.15 = (bf16[128,128]{1,0:T(8,128)(2,1)S(1)}, bf16[128,128]{1,0:T(8,128)(2,1)}, u32[]{:S(2)}) copy-start(bf16[128,128]{1,0:T(8,128)(2,1)} %get-tuple-element.124) | copy-start | bytes 98308
  62.2 15.6 %copy-start.16 = (bf16[128,128]{1,0:T(8,128)(2,1)S(1)}, bf16[128,128]{1,0:T(8,128)(2,1)}, u32[]{:S(2)}) copy-start(bf16[128,128]{1,0:T(8,128)(2,1)} %get-tuple-element.125) | copy-start | bytes 98308
  62.2 15.6 %copy-start.21 = (bf16[128,128]{1,0:T(8,128)(2,1)S(1)}, bf16[128,128]{1,0:T(8,128)(2,1)}, u32[]{:S(2)}) copy-start(bf16[128,128]{1,0:T(8,128)(2,1)} %get-tuple-element.126) | copy-start | bytes 98308
  62.3 15.6 %copy-start.22 = (bf16[128,128]{1,0:T(8,128)(2,1)S(1)}, bf16[128,128]{1,0:T(8,128)(2,1)}, u32[]{:S(2)}) copy-start(bf16[128,128]{1,0:T(8,128)(2,1)} %get-tuple-element.127) | copy-start | bytes 98308
  62.8 15.0 %collective-permute-start.1 = (bf16[2,128,1024]{2,1,0:T(8,128)(2,1)S(1)}, bf16[2,128,1024]{2,1,0:T(8,128)(2,1)S(1)}, u32[]{:S(2)}, u32[]{:S(2)}) collective-permute-start(bf16[2,128,1024]{2,1,0:T(8,128)(2,1)S(1)} %bitcast.233), channel_id=1, source_target_pairs={{0,4},{4,0},{8,12},{12,8},{16,20},{20,16},{24,28},{28,24},{32,36},... | collective-permute-start | bytes 1572872 | tf_op jit(solution)/shard_map/ppermute | solution.py:22
  78.3 28.0 %copy-start.13 = (bf16[128,128]{1,0:T(8,128)(2,1)S(1)}, bf16[128,128]{1,0:T(8,128)(2,1)}, u32[]{:S(2)}) copy-start(bf16[128,128]{1,0:T(8,128)(2,1)} %get-tuple-element.120) | copy-start | bytes 98308
  78.4 28.0 %copy-start.14 = (bf16[128,128]{1,0:T(8,128)(2,1)S(1)}, bf16[128,128]{1,0:T(8,128)(2,1)}, u32[]{:S(2)}) copy-start(bf16[128,128]{1,0:T(8,128)(2,1)} %get-tuple-element.121) | copy-start | bytes 98308
  78.4 28.0 %copy-start.19 = (bf16[128,128]{1,0:T(8,128)(2,1)S(1)}, bf16[128,128]{1,0:T(8,128)(2,1)}, u32[]{:S(2)}) copy-start(bf16[128,128]{1,0:T(8,128)(2,1)} %get-tuple-element.122) | copy-start | bytes 98308
  78.4 28.0 %copy-start.20 = (bf16[128,128]{1,0:T(8,128)(2,1)S(1)}, bf16[128,128]{1,0:T(8,128)(2,1)}, u32[]{:S(2)}) copy-start(bf16[128,128]{1,0:T(8,128)(2,1)} %get-tuple-element.123) | copy-start | bytes 98308
  78.4 28.0 %collective-permute-start.2 = (bf16[2,128,1024]{2,1,0:T(8,128)(2,1)S(1)}, bf16[2,128,1024]{2,1,0:T(8,128)(2,1)S(1)}, u32[]{:S(2)}, u32[]{:S(2)}) collective-permute-start(bf16[2,128,1024]{2,1,0:T(8,128)(2,1)S(1)} %bitcast.247), channel_id=1, source_target_pairs={{0,8},{8,0},{4,12},{12,4},{16,24},{24,16},{20,28},{28,20},{32,40},... | collective-permute-start | bytes 1572872 | tf_op jit(solution)/shard_map/ppermute | solution.py:22
  106.9 28.8 %copy-start.11 = (bf16[128,128]{1,0:T(8,128)(2,1)S(1)}, bf16[128,128]{1,0:T(8,128)(2,1)}, u32[]{:S(2)}) copy-start(bf16[128,128]{1,0:T(8,128)(2,1)} %get-tuple-element.116) | copy-start | bytes 98308
  106.9 28.8 %copy-start.12 = (bf16[128,128]{1,0:T(8,128)(2,1)S(1)}, bf16[128,128]{1,0:T(8,128)(2,1)}, u32[]{:S(2)}) copy-start(bf16[128,128]{1,0:T(8,128)(2,1)} %get-tuple-element.117) | copy-start | bytes 98308
  106.9 28.8 %copy-start.17 = (bf16[128,128]{1,0:T(8,128)(2,1)S(1)}, bf16[128,128]{1,0:T(8,128)(2,1)}, u32[]{:S(2)}) copy-start(bf16[128,128]{1,0:T(8,128)(2,1)} %get-tuple-element.118) | copy-start | bytes 98308
  106.9 28.8 %copy-start.18 = (bf16[128,128]{1,0:T(8,128)(2,1)S(1)}, bf16[128,128]{1,0:T(8,128)(2,1)}, u32[]{:S(2)}) copy-start(bf16[128,128]{1,0:T(8,128)(2,1)} %get-tuple-element.119) | copy-start | bytes 98308
  107.0 28.7 %collective-permute-start.3 = (bf16[2,128,1024]{2,1,0:T(8,128)(2,1)S(1)}, bf16[2,128,1024]{2,1,0:T(8,128)(2,1)S(1)}, u32[]{:S(2)}, u32[]{:S(2)}) collective-permute-start(bf16[2,128,1024]{2,1,0:T(8,128)(2,1)S(1)} %bitcast.248), channel_id=1, source_target_pairs={{0,16},{16,0},{4,20},{20,4},{8,24},{24,8},{12,28},{28,12},{32,48},... | collective-permute-start | bytes 1572872 | tf_op jit(solution)/shard_map/ppermute | solution.py:22
  136.2 14.6 %collective-permute-start.4 = (bf16[2,128,1024]{2,1,0:T(8,128)(2,1)S(1)}, bf16[2,128,1024]{2,1,0:T(8,128)(2,1)S(1)}, u32[]{:S(2)}, u32[]{:S(2)}) collective-permute-start(bf16[2,128,1024]{2,1,0:T(8,128)(2,1)S(1)} %bitcast.249), channel_id=1, source_target_pairs={{0,32},{32,0},{4,36},{36,4},{8,40},{40,8},{12,44},{44,12},{16,48},... | collective-permute-start | bytes 1572872 | tf_op jit(solution)/shard_map/ppermute | solution.py:22
  151.4 27.8 %collective-permute-start.5 = (bf16[2,128,1024]{2,1,0:T(8,128)(2,1)S(1)}, bf16[2,128,1024]{2,1,0:T(8,128)(2,1)S(1)}, u32[]{:S(2)}, u32[]{:S(2)}) collective-permute-start(bf16[2,128,1024]{2,1,0:T(8,128)(2,1)S(1)} %bitcast.250), channel_id=1, source_target_pairs={{0,64},{64,0},{4,68},{68,4},{8,72},{72,8},{12,76},{76,12},{16,80},... | collective-permute-start | bytes 1572872 | tf_op jit(solution)/shard_map/ppermute | solution.py:22
  (18 other events, 56.6 us)
where the time goes:
time: 181 us; the launch traced here: 180 us
  waiting for transfers between devices  103 us (57%)
  local copies, waits for them, and re-layouts  29.8 us (16%)
  starting transfers between devices  24.3 us (13%)
  matrix products  11.7 us (6%)
  other arithmetic  9.67 us (5%)
    ppermute x5, waiting for transfers between devices, from_partner(): return lax.ppermute(block, axis, route)  98.5 us
    unnamed x95, local copies, waits for them, and re-layouts  13.9 us
    ppermute x5, starting transfers between devices, from_partner(): return lax.ppermute(block, axis, route)  12.1 us
    ppermute x1, starting transfers between devices, from_behind(): return lax.ppermute(value, axis, pairs)  8.78 us
    all_to_all x1, waiting for transfers between devices, on_device(): lax.all_to_all(compressed, 'section', split_axis=2, concat_axis=1, tiled=...  4.89 us
    dot_general x10, matrix products, band_matrix(): jnp.einsum('sqt,tqc->sqc', coef_side, selector, preferred_element_type=jn...  4.58 us
  transfers between devices with their start and end apart: 7, of which 6 were waited for; matrix products, arithmetic and copies ran while one was open for 16% of the time, Pallas kernels for 0%

commit v1 on v0

--- a/solution.py
+++ b/solution.py
@@ -4,6 +4,29 @@
 from jax.sharding import PartitionSpec as P
 
 CBLK = 128
+
+
+def treat_task(xin, across):
+    all_rows = jax.lax.axis_size(across)
+    base_arr = jax.lax.axis_index(across)
+    block_now, shaped = (all_rows, base_arr)
+    tall = xin.shape[2] // block_now
+    right_arr = list(xin.shape)
+    right_arr[2] = tall
+    wide_out = right_arr[1]
+    right_arr[1] = wide_out * block_now
+    v_next = jnp.zeros(right_arr, xin.dtype)
+    for idx in range(block_now):
+        response = lax.dynamic_slice_in_dim(xin, (shaped ^ idx) * tall, tall, axis=2)
+        if idx:
+            store = []
+            for hop_no in range(block_now):
+                store.append((hop_no, hop_no ^ idx))
+            response = jax.lax.ppermute(response, across, store)
+        v_next = lax.dynamic_update_slice_in_dim(
+            v_next, response, (shaped ^ idx) * wide_out, axis=1
+        )
+    return v_next
 
 
 def from_behind(value, axis, by):
@@ -103,7 +126,7 @@
 
 def on_device(echoes, chirp, steer, pulse_order, band_coef, band_start, band_width):
     compressed = compress(echoes[:, 0], chirp)
-    pulse_rows = lax.all_to_all(compressed, "section", split_axis=2, concat_axis=1, tiled=True)
+    pulse_rows = treat_task(compressed, "section")
     position_count = pulse_order.shape[1]
     positions = jnp.arange(position_count, dtype=jnp.int32)
     selector = (positions[:, None] == pulse_order[0][None, :]).astype(jnp.bfloat16)

time: 181 us -> 173 us (0.956)
  local copies, waits for them, and re-layouts: 29.8 us -> 18.9 us
  starting transfers between devices: 24.3 us -> 31 us
  waiting for transfers between devices: 103 us -> 99.6 us
    ppermute x0 -> x3, starting transfers between devices: none -> 9.76 us  [treat_task(): response = jax.lax.ppermute(response, across, store)]
    unnamed x95 -> x93, local copies, waits for them, and re-layouts: 13.9 us -> 4.97 us
    all_to_all x1 -> x0, waiting for transfers between devices: 4.89 us -> none  [on_device(): lax.all_to_all(compressed, 'section', split_axis=2, concat_axis=1, tiled=...]
    all_to_all x1 -> x0, starting transfers between devices: 3.49 us -> none  [on_device(): lax.all_to_all(compressed, 'section', split_axis=2, concat_axis=1, tiled=...]
  transfers between devices with their start and end apart: 7 -> 9, of which waited for: 6 -> 6; matrix products, arithmetic and copies ran while one was open for 16% -> 17% of each run, Pallas kernels for 0% -> 0%
where the time goes in v1:
time: 173 us; the launch traced here: 172 us
  waiting for transfers between devices  99.6 us (58%)
  starting transfers between devices  31 us (18%)
  local copies, waits for them, and re-layouts  18.9 us (11%)
  matrix products  11.7 us (7%)
  other arithmetic  9.65 us (6%)
    ppermute x5, waiting for transfers between devices, from_partner(): return lax.ppermute(block, axis, route)  98.8 us
    ppermute x5, starting transfers between devices, from_partner(): return lax.ppermute(block, axis, route)  12.5 us
    ppermute x3, starting transfers between devices, treat_task(): response = jax.lax.ppermute(response, across, store)  9.76 us
    ppermute x1, starting transfers between devices, from_behind(): return lax.ppermute(value, axis, pairs)  8.78 us
    unnamed x93, local copies, waits for them, and re-layouts  4.97 us
    dot_general x10, matrix products, band_matrix(): jnp.einsum('sqt,tqc->sqc', coef_side, selector, preferred_element_type=jn...  4.58 us
    dot_general x17, matrix products, add_piece(): jnp.einsum('pbi,io->pbo', window, table, preferred_element_type=jnp.float32)  3.56 us
  transfers between devices with their start and end apart: 9, of which 6 were waited for; matrix products, arithmetic and copies ran while one was open for 17% of the time, Pallas kernels for 0%

profile of v1, /device:TPU:1, one launch (start us, length us, event | category | flops | bytes accessed | tf_op | source)
XLA Modules:
  0.0 172.5 jit_solution(11453540824143393047)
XLA Ops:
  0.0 1.5 slice.435
  1.5 8.8 %collective-permute-start = (bf16[2,6,2048]{2,0,1:T(2,128)(2,1)}, bf16[2,6,2048]{2,0,1:T(2,128)(2,1)}, u32[]{:S(2)}, u32[]{:S(2)}) collective-permute-start(bf16[2,6,2048]{2,0,1:T(2,128)(2,1)} %slice.435), channel_id=1, source_target_pairs={{1,0},{2,1},{3,2},{5,4},{6,5},{7,6},{9,8},{10,9},{11,10},{13,12},{... | collective-permute-start | bytes 147464 | tf_op jit(solution)/shard_map/ppermute | solution.py:35
  11.1 1.3 copy.144
  13.3 2.1 %reshape.578 = bf16[622336]{0:T(1024)(128)(2,1)S(1)} reshape(bf16[2,311168]{1,0:T(2,128)(2,1)S(1)} %slice.436) | data formatting | bytes 2489344
  15.5 2.2 %reshape.574 = bf16[2,128,2431]{2,1,0:T(8,128)(2,1)S(1)} reshape(bf16[622336]{0:T(1024)(128)(2,1)S(1)} %reshape.578) | data formatting | bytes 2489344 | tf_op jit(solution)/shard_map/reshape | solution.py:85
  17.6 1.1 slice.437
  18.7 1.7 copy.106
  35.2 1.4 maximum_maximum_fusion
  36.7 1.1 maximum_bitcast_fusion
  37.9 4.0 %while.14 = (s32[]{:T(128)}, f32[6,32,256]{2,1,0:T(8,128)S(1)}, bf16[6,48,256]{2,1,0:T(8,128)(2,1)S(1)}, bf16[17,256,256]{2,1,0:T(8,128)(2,1)S(1)}, s32[]{:T(128)}, /*index=5*/s32[]{:T(128)}) while((s32[]{:T(128)}, f32[6,32,256]{2,1,0:T(8,128)S(1)}, bf16[6,48,256]{2,1,0:T(8,128)(2,1)S(1)}, bf16[17,256,256]{2,1,0:T(8,128)(2,1)S(1)}, ...), condition=%wide.region_1.2_spmd.clone, body=%wide.region_0.1_spmd.clone.sunk | while | flops 25264132 | bytes 623695 | solution.py:116
  42.1 1.9 %collective-permute-start.1 = (bf16[2,6,1024]{2,0,1:T(2,128)(2,1)S(1)}, bf16[2,6,1024]{2,0,1:T(2,128)(2,1)S(1)}, u32[]{:S(2)}, u32[]{:S(2)}) collective-permute-start(bf16[2,6,1024]{2,0,1:T(2,128)(2,1)S(1)} %get-tuple-element.144), channel_id=1, source_target_pairs={{0,128},{128,0},{256,384},{384,256},{1,129},{129,1},{257,385},{385... | collective-permute-start | bytes 73736 | tf_op jit(solution)/shard_map/ppermute | solution.py:25
  44.0 2.1 %collective-permute-start.2 = (bf16[2,6,1024]{2,0,1:T(2,128)(2,1)S(1)}, bf16[2,6,1024]{2,0,1:T(2,128)(2,1)S(1)}, u32[]{:S(2)}, u32[]{:S(2)}) collective-permute-start(bf16[2,6,1024]{2,0,1:T(2,128)(2,1)S(1)} %get-tuple-element.143), channel_id=1, source_target_pairs={{0,256},{128,384},{256,0},{384,128},{1,257},{129,385},{257,1},{385... | collective-permute-start | bytes 73736 | tf_op jit(solution)/shard_map/ppermute | solution.py:25
  46.1 5.7 %collective-permute-start.3 = (bf16[2,6,1024]{2,0,1:T(2,128)(2,1)S(1)}, bf16[2,6,1024]{2,0,1:T(2,128)(2,1)S(1)}, u32[]{:S(2)}, u32[]{:S(2)}) collective-permute-start(bf16[2,6,1024]{2,0,1:T(2,128)(2,1)S(1)} %get-tuple-element.142), channel_id=1, source_target_pairs={{0,384},{128,256},{256,128},{384,0},{1,385},{129,257},{257,129},{3... | collective-permute-start | bytes 73736 | tf_op jit(solution)/shard_map/ppermute | solution.py:25
  54.1 1.9 %collective-permute-start.4 = (bf16[2,128,1024]{2,1,0:T(8,128)(2,1)S(1)}, bf16[2,128,1024]{2,1,0:T(8,128)(2,1)S(1)}, u32[]{:S(2)}, u32[]{:S(2)}) collective-permute-start(bf16[2,128,1024]{2,1,0:T(8,128)(2,1)S(1)} %bitcast.234), channel_id=1, source_target_pairs={{0,4},{4,0},{8,12},{12,8},{16,20},{20,16},{24,28},{28,24},{32,36},... | collective-permute-start | bytes 1572872 | tf_op jit(solution)/shard_map/ppermute | solution.py:45
  56.9 12.1 %collective-permute-done.4 = bf16[2,128,1024]{2,1,0:T(8,128)(2,1)S(1)} collective-permute-done((bf16[2,128,1024]{2,1,0:T(8,128)(2,1)S(1)}, bf16[2,128,1024]{2,1,0:T(8,128)(2,1)S(1)}, u32[]{:S(2)}, u32[]{:S(2)}) %collective-permute-start.4) | collective-permute-done | bytes 524320 | tf_op jit(solution)/shard_map/ppermute | solution.py:45
  69.6 2.1 %collective-permute-start.5 = (bf16[2,128,1024]{2,1,0:T(8,128)(2,1)S(1)}, bf16[2,128,1024]{2,1,0:T(8,128)(2,1)S(1)}, u32[]{:S(2)}, u32[]{:S(2)}) collective-permute-start(bf16[2,128,1024]{2,1,0:T(8,128)(2,1)S(1)} %bitcast.247), channel_id=1, source_target_pairs={{0,8},{8,0},{4,12},{12,4},{16,24},{24,16},{20,28},{28,20},{32,40},... | collective-permute-start | bytes 1572872 | tf_op jit(solution)/shard_map/ppermute | solution.py:45
  72.4 25.1 %collective-permute-done.5 = bf16[2,128,1024]{2,1,0:T(8,128)(2,1)S(1)} collective-permute-done((bf16[2,128,1024]{2,1,0:T(8,128)(2,1)S(1)}, bf16[2,128,1024]{2,1,0:T(8,128)(2,1)S(1)}, u32[]{:S(2)}, u32[]{:S(2)}) %collective-permute-start.5) | collective-permute-done | bytes 524320 | tf_op jit(solution)/shard_map/ppermute | solution.py:45
  98.2 3.5 %collective-permute-start.6 = (bf16[2,128,1024]{2,1,0:T(8,128)(2,1)S(1)}, bf16[2,128,1024]{2,1,0:T(8,128)(2,1)S(1)}, u32[]{:S(2)}, u32[]{:S(2)}) collective-permute-start(bf16[2,128,1024]{2,1,0:T(8,128)(2,1)S(1)} %bitcast.248), channel_id=1, source_target_pairs={{0,16},{16,0},{4,20},{20,4},{8,24},{24,8},{12,28},{28,12},{32,48},... | collective-permute-start | bytes 1572872 | tf_op jit(solution)/shard_map/ppermute | solution.py:45
  102.6 25.0 %collective-permute-done.6 = bf16[2,128,1024]{2,1,0:T(8,128)(2,1)S(1)} collective-permute-done((bf16[2,128,1024]{2,1,0:T(8,128)(2,1)S(1)}, bf16[2,128,1024]{2,1,0:T(8,128)(2,1)S(1)}, u32[]{:S(2)}, u32[]{:S(2)}) %collective-permute-start.6) | collective-permute-done | bytes 524320 | tf_op jit(solution)/shard_map/ppermute | solution.py:45
  128.1 1.9 %collective-permute-start.7 = (bf16[2,128,1024]{2,1,0:T(8,128)(2,1)S(1)}, bf16[2,128,1024]{2,1,0:T(8,128)(2,1)S(1)}, u32[]{:S(2)}, u32[]{:S(2)}) collective-permute-start(bf16[2,128,1024]{2,1,0:T(8,128)(2,1)S(1)} %bitcast.249), channel_id=1, source_target_pairs={{0,32},{32,0},{4,36},{36,4},{8,40},{40,8},{12,44},{44,12},{16,48},... | collective-permute-start | bytes 1572872 | tf_op jit(solution)/shard_map/ppermute | solution.py:45
  130.8 12.2 %collective-permute-done.7 = bf16[2,128,1024]{2,1,0:T(8,128)(2,1)S(1)} collective-permute-done((bf16[2,128,1024]{2,1,0:T(8,128)(2,1)S(1)}, bf16[2,128,1024]{2,1,0:T(8,128)(2,1)S(1)}, u32[]{:S(2)}, u32[]{:S(2)}) %collective-permute-start.7) | collective-permute-done | bytes 524320 | tf_op jit(solution)/shard_map/ppermute | solution.py:45
  143.5 3.0 %collective-permute-start.8 = (bf16[2,128,1024]{2,1,0:T(8,128)(2,1)S(1)}, bf16[2,128,1024]{2,1,0:T(8,128)(2,1)S(1)}, u32[]{:S(2)}, u32[]{:S(2)}) collective-permute-start(bf16[2,128,1024]{2,1,0:T(8,128)(2,1)S(1)} %bitcast.250), channel_id=1, source_target_pairs={{0,64},{64,0},{4,68},{68,4},{8,72},{72,8},{12,76},{76,12},{16,80},... | collective-permute-start | bytes 1572872 | tf_op jit(solution)/shard_map/ppermute | solution.py:45
  146.7 24.4 %collective-permute-done.8 = bf16[2,128,1024]{2,1,0:T(8,128)(2,1)S(1)} collective-permute-done((bf16[2,128,1024]{2,1,0:T(8,128)(2,1)S(1)}, bf16[2,128,1024]{2,1,0:T(8,128)(2,1)S(1)}, u32[]{:S(2)}, u32[]{:S(2)}) %collective-permute-start.8) | collective-permute-done | bytes 524320 | tf_op jit(solution)/shard_map/ppermute | solution.py:45
  171.2 1.2 convolution_convert_fusion
  (191 shorter events, 27.5 us)
Async XLA Ops:
  0.0 21.4 %copy-start = (bf16[2,1,128,24]{2,3,1,0:T(8,128)(2,1)S(1)}, bf16[2,1,128,24]{2,3,1,0:T(8,128)(2,1)}, u32[]{:S(2)}) copy-start(bf16[2,1,128,24]{2,3,1,0:T(8,128)(2,1)} %param.11) | copy-start | bytes 36868
  1.5 35.3 %collective-permute-start = (bf16[2,6,2048]{2,0,1:T(2,128)(2,1)}, bf16[2,6,2048]{2,0,1:T(2,128)(2,1)}, u32[]{:S(2)}, u32[]{:S(2)}) collective-permute-start(bf16[2,6,2048]{2,0,1:T(2,128)(2,1)} %slice.435), channel_id=1, source_target_pairs={{1,0},{2,1},{3,2},{5,4},{6,5},{7,6},{9,8},{10,9},{11,10},{13,12},{... | collective-permute-start | bytes 147464 | tf_op jit(solution)/shard_map/ppermute | solution.py:35
  37.9 15.8 %copy-start.25 = (bf16[128,24]{0,1:T(8,128)(2,1)S(1)}, bf16[128,24]{0,1:T(8,128)(2,1)}, u32[]{:S(2)}) copy-start(bf16[128,24]{0,1:T(8,128)(2,1)} %get-tuple-element.176) | copy-start | bytes 18436
  37.9 18.2 %copy-start.3 = (bf16[1,128,128]{2,0,1:T(2,128)(2,1)S(1)}, bf16[1,128,128]{2,0,1:T(2,128)(2,1)}, u32[]{:S(2)}) copy-start(bf16[1,128,128]{2,0,1:T(2,128)(2,1)} %get-tuple-element.175) | copy-start | bytes 98308
  42.1 10.1 %collective-permute-start.1 = (bf16[2,6,1024]{2,0,1:T(2,128)(2,1)S(1)}, bf16[2,6,1024]{2,0,1:T(2,128)(2,1)S(1)}, u32[]{:S(2)}, u32[]{:S(2)}) collective-permute-start(bf16[2,6,1024]{2,0,1:T(2,128)(2,1)S(1)} %get-tuple-element.144), channel_id=1, source_target_pairs={{0,128},{128,0},{256,384},{384,256},{1,129},{129,1},{257,385},{385... | collective-permute-start | bytes 73736 | tf_op jit(solution)/shard_map/ppermute | solution.py:25
  44.0 8.5 %collective-permute-start.2 = (bf16[2,6,1024]{2,0,1:T(2,128)(2,1)S(1)}, bf16[2,6,1024]{2,0,1:T(2,128)(2,1)S(1)}, u32[]{:S(2)}, u32[]{:S(2)}) collective-permute-start(bf16[2,6,1024]{2,0,1:T(2,128)(2,1)S(1)} %get-tuple-element.143), channel_id=1, source_target_pairs={{0,256},{128,384},{256,0},{384,128},{1,257},{129,385},{257,1},{385... | collective-permute-start | bytes 73736 | tf_op jit(solution)/shard_map/ppermute | solution.py:25
  46.1 7.4 %collective-permute-start.3 = (bf16[2,6,1024]{2,0,1:T(2,128)(2,1)S(1)}, bf16[2,6,1024]{2,0,1:T(2,128)(2,1)S(1)}, u32[]{:S(2)}, u32[]{:S(2)}) collective-permute-start(bf16[2,6,1024]{2,0,1:T(2,128)(2,1)S(1)} %get-tuple-element.142), channel_id=1, source_target_pairs={{0,384},{128,256},{256,128},{384,0},{1,385},{129,257},{257,129},{3... | collective-permute-start | bytes 73736 | tf_op jit(solution)/shard_map/ppermute | solution.py:25
  52.0 17.0 %copy-start.15 = (bf16[128,128]{1,0:T(8,128)(2,1)S(1)}, bf16[128,128]{1,0:T(8,128)(2,1)}, u32[]{:S(2)}) copy-start(bf16[128,128]{1,0:T(8,128)(2,1)} %get-tuple-element.124) | copy-start | bytes 98308
  52.0 17.0 %copy-start.16 = (bf16[128,128]{1,0:T(8,128)(2,1)S(1)}, bf16[128,128]{1,0:T(8,128)(2,1)}, u32[]{:S(2)}) copy-start(bf16[128,128]{1,0:T(8,128)(2,1)} %get-tuple-element.125) | copy-start | bytes 98308
  52.0 17.0 %copy-start.21 = (bf16[128,128]{1,0:T(8,128)(2,1)S(1)}, bf16[128,128]{1,0:T(8,128)(2,1)}, u32[]{:S(2)}) copy-start(bf16[128,128]{1,0:T(8,128)(2,1)} %get-tuple-element.126) | copy-start | bytes 98308
  52.0 17.0 %copy-start.22 = (bf16[128,128]{1,0:T(8,128)(2,1)S(1)}, bf16[128,128]{1,0:T(8,128)(2,1)}, u32[]{:S(2)}) copy-start(bf16[128,128]{1,0:T(8,128)(2,1)} %get-tuple-element.127) | copy-start | bytes 98308
  54.1 14.9 %collective-permute-start.4 = (bf16[2,128,1024]{2,1,0:T(8,128)(2,1)S(1)}, bf16[2,128,1024]{2,1,0:T(8,128)(2,1)S(1)}, u32[]{:S(2)}, u32[]{:S(2)}) collective-permute-start(bf16[2,128,1024]{2,1,0:T(8,128)(2,1)S(1)} %bitcast.234), channel_id=1, source_target_pairs={{0,4},{4,0},{8,12},{12,8},{16,20},{20,16},{24,28},{28,24},{32,36},... | collective-permute-start | bytes 1572872 | tf_op jit(solution)/shard_map/ppermute | solution.py:45
  69.6 28.0 %copy-start.13 = (bf16[128,128]{1,0:T(8,128)(2,1)S(1)}, bf16[128,128]{1,0:T(8,128)(2,1)}, u32[]{:S(2)}) copy-start(bf16[128,128]{1,0:T(8,128)(2,1)} %get-tuple-element.120) | copy-start | bytes 98308
  69.6 28.0 %copy-start.14 = (bf16[128,128]{1,0:T(8,128)(2,1)S(1)}, bf16[128,128]{1,0:T(8,128)(2,1)}, u32[]{:S(2)}) copy-start(bf16[128,128]{1,0:T(8,128)(2,1)} %get-tuple-element.121) | copy-start | bytes 98308
  69.6 28.0 %copy-start.19 = (bf16[128,128]{1,0:T(8,128)(2,1)S(1)}, bf16[128,128]{1,0:T(8,128)(2,1)}, u32[]{:S(2)}) copy-start(bf16[128,128]{1,0:T(8,128)(2,1)} %get-tuple-element.122) | copy-start | bytes 98308
  69.6 28.0 %copy-start.20 = (bf16[128,128]{1,0:T(8,128)(2,1)S(1)}, bf16[128,128]{1,0:T(8,128)(2,1)}, u32[]{:S(2)}) copy-start(bf16[128,128]{1,0:T(8,128)(2,1)} %get-tuple-element.123) | copy-start | bytes 98308
  69.6 28.0 %collective-permute-start.5 = (bf16[2,128,1024]{2,1,0:T(8,128)(2,1)S(1)}, bf16[2,128,1024]{2,1,0:T(8,128)(2,1)S(1)}, u32[]{:S(2)}, u32[]{:S(2)}) collective-permute-start(bf16[2,128,1024]{2,1,0:T(8,128)(2,1)S(1)} %bitcast.247), channel_id=1, source_target_pairs={{0,8},{8,0},{4,12},{12,4},{16,24},{24,16},{20,28},{28,20},{32,40},... | collective-permute-start | bytes 1572872 | tf_op jit(solution)/shard_map/ppermute | solution.py:45
  98.1 29.5 %copy-start.11 = (bf16[128,128]{1,0:T(8,128)(2,1)S(1)}, bf16[128,128]{1,0:T(8,128)(2,1)}, u32[]{:S(2)}) copy-start(bf16[128,128]{1,0:T(8,128)(2,1)} %get-tuple-element.116) | copy-start | bytes 98308
  98.1 29.5 %copy-start.12 = (bf16[128,128]{1,0:T(8,128)(2,1)S(1)}, bf16[128,128]{1,0:T(8,128)(2,1)}, u32[]{:S(2)}) copy-start(bf16[128,128]{1,0:T(8,128)(2,1)} %get-tuple-element.117) | copy-start | bytes 98308
  98.1 29.5 %copy-start.17 = (bf16[128,128]{1,0:T(8,128)(2,1)S(1)}, bf16[128,128]{1,0:T(8,128)(2,1)}, u32[]{:S(2)}) copy-start(bf16[128,128]{1,0:T(8,128)(2,1)} %get-tuple-element.118) | copy-start | bytes 98308
  98.1 29.5 %copy-start.18 = (bf16[128,128]{1,0:T(8,128)(2,1)S(1)}, bf16[128,128]{1,0:T(8,128)(2,1)}, u32[]{:S(2)}) copy-start(bf16[128,128]{1,0:T(8,128)(2,1)} %get-tuple-element.119) | copy-start | bytes 98308
  98.2 29.4 %collective-permute-start.6 = (bf16[2,128,1024]{2,1,0:T(8,128)(2,1)S(1)}, bf16[2,128,1024]{2,1,0:T(8,128)(2,1)S(1)}, u32[]{:S(2)}, u32[]{:S(2)}) collective-permute-start(bf16[2,128,1024]{2,1,0:T(8,128)(2,1)S(1)} %bitcast.248), channel_id=1, source_target_pairs={{0,16},{16,0},{4,20},{20,4},{8,24},{24,8},{12,28},{28,12},{32,48},... | collective-permute-start | bytes 1572872 | tf_op jit(solution)/shard_map/ppermute | solution.py:45
  128.1 14.9 %collective-permute-start.7 = (bf16[2,128,1024]{2,1,0:T(8,128)(2,1)S(1)}, bf16[2,128,1024]{2,1,0:T(8,128)(2,1)S(1)}, u32[]{:S(2)}, u32[]{:S(2)}) collective-permute-start(bf16[2,128,1024]{2,1,0:T(8,128)(2,1)S(1)} %bitcast.249), channel_id=1, source_target_pairs={{0,32},{32,0},{4,36},{36,4},{8,40},{40,8},{12,44},{44,12},{16,48},... | collective-permute-start | bytes 1572872 | tf_op jit(solution)/shard_map/ppermute | solution.py:45
  143.5 27.7 %collective-permute-start.8 = (bf16[2,128,1024]{2,1,0:T(8,128)(2,1)S(1)}, bf16[2,128,1024]{2,1,0:T(8,128)(2,1)S(1)}, u32[]{:S(2)}, u32[]{:S(2)}) collective-permute-start(bf16[2,128,1024]{2,1,0:T(8,128)(2,1)S(1)} %bitcast.250), channel_id=1, source_target_pairs={{0,64},{64,0},{4,68},{68,4},{8,72},{72,8},{12,76},{76,12},{16,80},... | collective-permute-start | bytes 1572872 | tf_op jit(solution)/shard_map/ppermute | solution.py:45
  (20 other events, 126.2 us)
